TPU v7x, 32 devices: a whole 2x2x4 slice. The times are simulated.
32 devices in a mesh: section: 4 (over z), ctx: 8 (over y, x, core).
Axes of the slice: x: 2, y: 2, z: 4, core: 2. Of those that a mesh axis runs over, the one named last changes fastest.
Arguments:
- query: bfloat16 [4, 3072, 3072], P('section', 'ctx'), may hold values from -200 to 200
- key: bfloat16 [4, 3072, 3072], P('section', 'ctx'), may hold values from -6 to 6
- value: bfloat16 [4, 3072, 3072], P('section', 'ctx'), may hold values from -6 to 6
- out_grad: bfloat16 [4, 3072, 3072], P('section', 'ctx'), may hold values from -6 to 6
- tile_mask: int32 [16, 8], P('ctx'), may hold values from 0 to 1, as said below
Outputs:
- key_grad: bfloat16 [4, 3072, 3072], P('section', 'ctx')
- value_grad: bfloat16 [4, 3072, 3072], P('section', 'ctx')
- upstream: bfloat16 [4, 3072, 3072], P('section', 'ctx')
Inputs may be any that keep to these rules, and one draw needn't show every extreme that they name: `tile_mask`: every query tile a reads the key tile a // 2 of its own image rows; the share of ones differs from one pair of query tiles to the next.
All inputs are finite; a program needn't handle non-finite values.
Results may differ from a plain program's by a relative error of at most 0.014.
The roundings to bfloat16 on the way count: a program that leaves them out, or rounds other values in their place, can miss the bound.
Values may be sent and summed in bfloat16 or wider, within the bound.
A program may use at most 256 MiB of HBM per device.

v0:
```python
import jax
import jax.numpy as jnp
from jax import lax
from jax.sharding import PartitionSpec as P

HD = 128


def from_behind(value, axis, steps):
    count = lax.axis_size(axis)
    first, last = (max(0, -steps), min(count, count - steps))
    return lax.ppermute(value, axis, [(source, source + steps) for source in range(first, last)])


def pool_band(data, width):
    count = data.shape[0] // (2 * width)
    grid = data.astype(jnp.float32).reshape(count, 2, width // 2, 2, data.shape[1])
    return grid.mean(axis=(1, 3)).reshape(-1, data.shape[1]).astype(jnp.bfloat16)


def unpool_band(pooled, width):
    grid = (pooled / 4.0).reshape(1, 1, width // 2, 1, pooled.shape[1])
    grid = jnp.broadcast_to(grid, (1, 2, width // 2, 2, pooled.shape[1]))
    return grid.reshape(-1, pooled.shape[1]).astype(jnp.bfloat16)


def head_core(qhead, khead, vhead, dhead, allowed):
    scale = 1.0 / HD**0.5
    scores = jnp.dot(qhead, khead.T, preferred_element_type=jnp.float32) * scale
    scores = jnp.where(allowed, scores, -1e30)
    top = jnp.max(scores, axis=1, keepdims=True)
    expo = jnp.exp(scores - top)
    probs = expo / jnp.sum(expo, axis=1, keepdims=True)
    probs_low = probs.astype(jnp.bfloat16)
    attended = jnp.dot(probs_low, vhead, preferred_element_type=jnp.float32)
    delta = jnp.sum(dhead.astype(jnp.float32) * attended, axis=1, keepdims=True)
    dprob = jnp.dot(dhead, vhead.T, preferred_element_type=jnp.float32)
    score_grad = (probs * (dprob - delta) * scale).astype(jnp.bfloat16)
    qgrad = jnp.dot(score_grad, khead, preferred_element_type=jnp.float32).astype(jnp.bfloat16)
    return (qgrad, score_grad, probs_low)


def shards(query, key, value, out_grad, tile_mask):
    local_q = query[0]
    local_k = key[0]
    local_v = value[0]
    local_d = out_grad[0]
    tokens, width_all = local_q.shape
    row_len = tokens // 2
    pooled_key, pooled_value = (
        lax.all_gather(pool_band(local_k, row_len), "ctx", axis=0, tiled=True),
        lax.all_gather(pool_band(local_v, row_len), "ctx", axis=0, tiled=True),
    )
    rows_mask = jnp.repeat(tile_mask, row_len, axis=0)
    allowed = jnp.repeat(rows_mask, row_len // 2, axis=1) > 0
    heads = width_all // HD

    def head_slices(index):
        start = index * HD
        qh = lax.dynamic_slice_in_dim(local_q, start, HD, 1)
        kh = lax.dynamic_slice_in_dim(pooled_key, start, HD, 1)
        vh = lax.dynamic_slice_in_dim(pooled_value, start, HD, 1)
        dh = lax.dynamic_slice_in_dim(local_d, start, HD, 1)
        return (qh, kh, vh, dh)

    def per_head_kept(index):
        qh, kh, vh, dh = head_slices(index)
        return head_core(qh, kh, vh, dh, allowed)

    qgrad, score_all, probs_all = lax.map(per_head_kept, jnp.arange(heads, dtype=jnp.int32))
    qgrad = jnp.transpose(qgrad, (1, 0, 2)).reshape(tokens, width_all)
    query_heads = local_q.reshape(tokens, heads, HD)
    grad_heads = local_d.reshape(tokens, heads, HD)
    kpart = jnp.einsum("htk,thd->khd", score_all, query_heads, preferred_element_type=jnp.float32)
    vpart = jnp.einsum("htk,thd->khd", probs_all, grad_heads, preferred_element_type=jnp.float32)
    summed = lax.psum_scatter(
        jnp.concatenate(
            [
                kpart.reshape(row_len // 2 * lax.axis_size("ctx"), width_all),
                vpart.reshape(row_len // 2 * lax.axis_size("ctx"), width_all),
            ],
            axis=1,
        ).astype(jnp.bfloat16),
        "ctx",
        scatter_dimension=0,
        tiled=True,
    ).astype(jnp.float32)
    kgrad = summed[:, :width_all]
    vgrad = summed[:, width_all:]
    upstream = from_behind(qgrad, "section", -1)
    key_grad = unpool_band(kgrad, row_len)
    value_grad = unpool_band(vgrad, row_len)
    return (key_grad[None], value_grad[None], upstream[None])


def solution(mesh):
    return jax.shard_map(
        shards,
        mesh=mesh,
        in_specs=(
            P("section", "ctx", None),
            P("section", "ctx", None),
            P("section", "ctx", None),
            P("section", "ctx", None),
            P("ctx", None),
        ),
        out_specs=(P("section", "ctx", None), P("section", "ctx", None), P("section", "ctx", None)),
        check_vma=False,
    )
```

profile of v0, /device:TPU:1, one launch (start us, length us, event | category | flops | bytes accessed | tf_op | source)
XLA Modules:
  0.0 484.1 jit_solution(11086844435602450511)
XLA Ops:
  7.2 6.1 %reshape.109 = f32[2,96,2,3072]{3,2,1,0:T(2,128)} reshape(bf16[1,384,3072]{2,1,0:T(8,128)(2,1)} %param.8) | data formatting | bytes 7077888 | tf_op jit(solution)/shard_map/convert_element_type | solution.py:17
  13.3 5.7 %reduce_sum.36 = f32[96,3072]{1,0:T(8,128)S(1)} reduce(f32[2,96,2,3072]{3,2,1,0:T(2,128)} %reshape.109, f32[]{:T(128)} %constant.37.clone.1), dimensions={0,2}, to_apply=%region_0.0 | reduce | flops 884736 | bytes 5898244 | tf_op jit(solution)/shard_map/reduce_sum | solution.py:18
  20.9 4.3 reshape.110
  25.2 5.7 %reduce_sum.37 = f32[96,3072]{1,0:T(8,128)S(1)} reduce(f32[2,96,2,3072]{3,2,1,0:T(2,128)} %reshape.110, f32[]{:T(128)} %constant.37.clone.1), dimensions={0,2}, to_apply=%region_1.0 | reduce | flops 884736 | bytes 5898244 | tf_op jit(solution)/shard_map/reduce_sum | solution.py:18
  32.1 3.0 copy.23
  35.4 4.3 copy.30
  39.7 21.7 %all-gather.3.cloned.1.call-done = bf16[768,3072]{1,0:T(8,128)(2,1)} async-done(((bf16[96,3072]{1,0:T(8,128)(2,1)}), bf16[768,3072]{1,0:T(8,128)(2,1)}) %all-gather.3.cloned.1.call-update) | async-done | bytes 4718608 | tf_op jit(solution)/shard_map/all_gather | solution.py:51
  61.4 40.7 %all-gather.5.cloned.1.call-done = bf16[768,3072]{1,0:T(8,128)(2,1)} async-done(((bf16[96,3072]{1,0:T(8,128)(2,1)}), bf16[768,3072]{1,0:T(8,128)(2,1)}) %all-gather.5.cloned.1.call-update) | async-done | bytes 4718608 | tf_op jit(solution)/shard_map/all_gather | solution.py:52
  102.1 245.0 %while.15 = (s32[]{:T(128)}, bf16[24,384,128]{2,1,0:T(8,128)(2,1)}, bf16[24,384,768]{2,1,0:T(8,128)(2,1)}, bf16[24,384,768]{2,1,0:T(8,128)(2,1)}, s32[24]{0:T(12...) while((s32[]{:T(128)}, bf16[24,384,128]{2,1,0:T(8,128)(2,1)}, ...), condition=%wide.region_6.7_spmd.clone, body=%wide.region_2.6_spmd.clone.sunk | while | flops 307198848 | bytes 10643139 | solution.py:70
  128.5 2.3 bitcast_dynamic-update-slice_fusion.4
  199.9 2.3 bitcast_dynamic-update-slice_fusion.4
  250.9 2.3 bitcast_dynamic-update-slice_fusion.4
  261.2 2.3 bitcast_dynamic-update-slice_fusion.4
  332.7 2.3 bitcast_dynamic-update-slice_fusion.4
  347.0 9.8 %convolution_convert_fusion.1 = bf16[24,768,128]{1,2,0:T(8,128)(2,1)} fusion(bf16[384,24,128]{0,2,1:T(8,128)(2,1)S(1)} %bitcast.50, bf16[24,384,768]{2,1,0:T(8,128)(2,1)} %get-tuple-element.58), kind=kOutput, calls=%fused_computation.29 | convolution fusion | flops 1814298624 | bytes 21233664 | tf_op jit(solution)/shard_map/htk,thd->khd/dot_general | solution.py:75
  356.8 6.8 %copy.28 = bf16[768,3072]{1,0:T(8,128)(2,1)} copy(bf16[768,3072]{0,1:T(8,128)(2,1)} %bitcast.46) | data formatting | bytes 9437184 | tf_op jit(solution)/shard_map/reshape | solution.py:80
  363.7 9.8 %convolution_convert_fusion.2 = bf16[24,768,128]{1,2,0:T(8,128)(2,1)} fusion(bf16[384,24,128]{0,2,1:T(8,128)(2,1)S(1)} %bitcast.51, bf16[24,384,768]{2,1,0:T(8,128)(2,1)} %get-tuple-element.57), kind=kOutput, calls=%fused_computation.30 | convolution fusion | flops 1814298624 | bytes 21233664 | tf_op jit(solution)/shard_map/htk,thd->khd/dot_general | solution.py:74
  373.5 6.6 %copy.27 = bf16[768,3072]{1,0:T(8,128)(2,1)} copy(bf16[768,3072]{0,1:T(8,128)(2,1)} %bitcast.47) | data formatting | bytes 9437184 | tf_op jit(solution)/shard_map/reshape | solution.py:79
  380.1 9.1 %pad_maximum_fusion = bf16[768,6144]{1,0:T(8,128)(2,1)} fusion(bf16[768,3072]{1,0:T(8,128)(2,1)} %copy.28, bf16[768,3072]{1,0:T(8,128)(2,1)} %copy.27), kind=kLoop, calls=%fused_computation.28 | loop fusion | flops 18874368 | bytes 18874368 | tf_op jit(solution)/shard_map/concatenate | solution.py:77
  392.7 53.0 %collective-permute-done = bf16[384,3072]{1,0:T(8,128)(2,1)} collective-permute-done((bf16[384,3072]{1,0:T(8,128)(2,1)S(1)}, bf16[384,3072]{1,0:T(8,128)(2,1)}, u32[]{:S(2)}, u32[]{:S(2)}) %collective-permute-start) | collective-permute-done | bytes 2359328 | tf_op jit(solution)/shard_map/ppermute | solution.py:12
  445.8 19.8 %reduce-scatter.2.cloned.1.call-done = bf16[96,6144]{1,0:T(8,128)(2,1)} async-done(((bf16[768,6144]{1,0:T(8,128)(2,1)}), bf16[96,6144]{1,0:T(8,128)(2,1)}) %reduce-scatter.2.cloned.1.call-update) | async-done | bytes 1179664 | tf_op jit(solution)/shard_map/reduce_scatter | solution.py:76
  468.4 2.3 convert_element_type.90
  472.0 2.3 convert_element_type.92
  474.3 3.2 copy.53
  (241 shorter events, 228.1 us)
Async XLA Ops:
  7.2 54.2 %all-gather.3.cloned.1.call-start = ((), (), s32[]{:S(2)}) async-start(), calls=%async_computation.1 | async-start | bytes 5308416 | tf_op jit(solution)/shard_map/all_gather | solution.py:51
  19.0 1.9 copy-start.1
  20.0 82.1 %all-gather.5.cloned.1.call-start = ((), (), s32[]{:S(2)}) async-start(), calls=%async_computation.2 | async-start | bytes 5308416 | tf_op jit(solution)/shard_map/all_gather | solution.py:52
  31.8 433.8 %reduce-scatter.2.cloned.1.call-start = ((), (), s32[]{:S(2)}) async-start(), calls=%async_computation.3 | async-start | bytes 10616832 | tf_op jit(solution)/shard_map/reduce_scatter | solution.py:76
  32.1 3.0 copy-start.3
  356.8 6.8 %copy-start = (bf16[1,384,3072]{1,2,0:T(8,128)(2,1)S(1)}, bf16[1,384,3072]{1,2,0:T(8,128)(2,1)}, u32[]{:S(2)}) copy-start(bf16[1,384,3072]{1,2,0:T(8,128)(2,1)} %copy.30) | copy-start | bytes 7077892
  389.2 1.7 copy-start.2
  391.2 54.6 %collective-permute-start = (bf16[384,3072]{1,0:T(8,128)(2,1)S(1)}, bf16[384,3072]{1,0:T(8,128)(2,1)}, u32[]{:S(2)}, u32[]{:S(2)}) collective-permute-start(bf16[384,3072]{1,0:T(8,128)(2,1)S(1)} %copy_bitcast_fusion), channel_id=1, source_target_pairs={{8,0},{16,8},{24,16},{9,1},{17,9},{25,17},{10,2},{18,10},{26,18},{... | collective-permute-start | bytes 7077896 | tf_op jit(solution)/shard_map/ppermute | solution.py:12
Sparse Core Ops, SparseCore 0:
  20.1 41.2 all-gather.2
  63.3 38.7 all-gather.4
  389.3 76.2 reduce-scatter.1
where the time goes:
time: 488 us; the launch traced here: 484 us
  matrix products  188 us (39%)
  waiting for transfers between devices  135 us (28%)
  local copies, waits for them, and re-layouts  69.6 us (14%)
  other arithmetic  59.3 us (12%)
  loops' own time  16.2 us (3%)
  between operations  13.9 us (3%)
    dot_general x24, matrix products, head_core(): dprob = jnp.dot(dhead, vhead.T, preferred_element_type=jnp.float32)  54.4 us
    ppermute x1, waiting for transfers between devices, from_behind(): lax.ppermute(value, axis, [(source, source + steps) for source in range(f...  53 us
    dot_general x24, matrix products, head_core(): jnp.dot(score_grad, khead, preferred_element_type=jnp.float32)  45.3 us
    all_gather x1, waiting for transfers between devices, shards(): lax.all_gather(pool_band(local_v, row_len), 'ctx', axis=0, tiled=True)  40.7 us
    dot_general x24, matrix products, head_core(): attended = jnp.dot(probs_low, vhead, preferred_element_type=jnp.float32)  34.7 us
    dot_general x24, matrix products, head_core(): scores = jnp.dot(qhead, khead.T, preferred_element_type=jnp.float32) * scale  34 us
    dynamic_update_slice x24, other arithmetic, shards(): lax.map(per_head_kept, jnp.arange(heads, dtype=jnp.int32))  26.9 us
    all_gather x1, waiting for transfers between devices, shards(): lax.all_gather(pool_band(local_k, row_len), 'ctx', axis=0, tiled=True)  21.7 us
  transfers between devices with their start and end apart: 4, of which 4 were waited for; matrix products, arithmetic and copies ran while one was open for 4% of the time, Pallas kernels for 0%

commit v1 on v0

v1 whole, which is shorter than its diff:
```python
import functools

import jax
import jax.numpy as jnp
from jax import lax
from jax.experimental import pallas as pl
from jax.experimental.pallas import tpu as pltpu
from jax.sharding import PartitionSpec as P

HD = 128
MESH = pl.DeviceIdType.MESH
LOG2E = 1.4426950408889634


def dot(a, b, dims):
    return lax.dot_general(a, b, (dims, ((), ())), preferred_element_type=jnp.float32)


def kernel(
    sections, count, groups, wide,
    q_hbm, k_hbm, v_hbm, d_hbm, bias_hbm,
    kg_hbm, vg_hbm, up_hbm,
    kin, pooled, kv, qd, bias, terms, arrived, dq,
    in_sem, own_sem, own_bias_sem, swap_send, swap_recv, bias_sems,
    kv_send, kv_recv, term_send, term_recv, dq_send, dq_recv, out_sem,
):
    tokens = qd.shape[3]
    row_len = tokens // 2
    pool = pooled.shape[3]
    section = lax.axis_index("section")
    me = lax.axis_index("ctx")
    core = lax.rem(me, 2)
    chip_first = me - core
    partner = chip_first + 1 - core

    def columns(half, g):
        return pl.ds(pl.multiple_of((half * groups + g) * wide, wide), wide)

    def in_copy(which, half, g):
        src = (k_hbm, v_hbm)[which]
        return pltpu.make_async_copy(
            src.at[0, :, columns(half, g)], kin.at[which, :, columns(half, g)], in_sem.at[which, half, g]
        )

    def own_copy(which, g):
        src = (q_hbm, d_hbm)[which]
        return pltpu.make_async_copy(src.at[0, :, columns(core, g)], qd.at[g, which, core], own_sem.at[which, g])

    def own_bias():
        return pltpu.make_async_copy(bias_hbm, bias.at[core], own_bias_sem)

    @pl.loop(0, groups)
    def _(g):
        for which in range(2):
            for half in range(2):
                in_copy(which, half, g).start()

    @pl.loop(0, groups)
    def _(g):
        for which in range(2):
            own_copy(which, g).start()

    own_bias().start()

    barrier = pltpu.get_barrier_semaphore()
    for step in range(1, count):
        pl.semaphore_signal(
            barrier, inc=1, device_id=(section, lax.rem(me + step, count)), device_id_type=MESH
        )

    @pl.when(section > 0)
    def _():
        for c in range(2):
            pl.semaphore_signal(barrier, inc=1, device_id=(section - 1, chip_first + c), device_id_type=MESH)

    @pl.when(section < sections - 1)
    def _():
        for c in range(2):
            pl.semaphore_signal(barrier, inc=1, device_id=(section + 1, chip_first + c), device_id_type=MESH)

    edges = jnp.where(section > 0, 2, 0) + jnp.where(section < sections - 1, 2, 0)
    pl.semaphore_wait(barrier, count - 1 + edges)

    def swap(which, g):
        src = (q_hbm, d_hbm)[which]
        return pltpu.make_async_remote_copy(
            src_ref=src.at[0, :, columns(1 - core, g)],
            dst_ref=qd.at[g, which, core],
            send_sem=swap_send.at[which, g],
            recv_sem=swap_recv.at[which, g],
            device_id=(section, partner),
            device_id_type=MESH,
        )

    def swap_bias():
        return pltpu.make_async_remote_copy(
            src_ref=bias_hbm,
            dst_ref=bias.at[core],
            send_sem=bias_sems.at[0],
            recv_sem=bias_sems.at[1],
            device_id=(section, partner),
            device_id_type=MESH,
        )

    swap_bias().start()

    @pl.loop(0, groups)
    def _(g):
        for which in range(2):
            swap(which, g).start()

    def kv_out(g, peer):
        return pltpu.make_async_remote_copy(
            src_ref=pooled.at[lax.rem(peer, 2), g],
            dst_ref=kv.at[g, me],
            send_sem=kv_send.at[g, peer],
            recv_sem=kv_recv.at[g, me],
            device_id=(section, peer),
            device_id_type=MESH,
        )

    def kv_in(g, peer):
        return pltpu.make_async_remote_copy(
            src_ref=pooled.at[core, g],
            dst_ref=kv.at[g, peer],
            send_sem=kv_send.at[g, peer],
            recv_sem=kv_recv.at[g, peer],
            device_id=(section, peer),
            device_id_type=MESH,
        )

    def pool_matrix(shape, token_dim, value):
        token = lax.broadcasted_iota(jnp.int32, shape, token_dim)
        token = jnp.where(token >= row_len, token - row_len, token)
        cell = lax.broadcasted_iota(jnp.int32, shape, 1 - token_dim)
        return jnp.where((token >> 1) == cell, value, 0.0).astype(jnp.bfloat16)

    @pl.loop(0, groups)
    def _(g):
        mean = pool_matrix((pool, tokens), 1, 0.25)
        for half in range(2):
            for which in range(2):
                in_copy(which, half, g).wait()
                block = dot(mean, kin[which, :, columns(half, g)], ((1,), (0,)))
                pooled[half, g, which] = block.astype(jnp.bfloat16)
        kv[g, me] = pooled[core, g]

        @pl.loop(1, count)
        def _(step):
            kv_out(g, lax.rem(me + step, count)).start()

    def term_out(g, peer):
        return pltpu.make_async_remote_copy(
            src_ref=terms.at[g, peer],
            dst_ref=arrived.at[g, me],
            send_sem=term_send.at[g, peer],
            recv_sem=term_recv.at[g, me],
            device_id=(section, peer),
            device_id_type=MESH,
        )

    def term_in(g, peer):
        return pltpu.make_async_remote_copy(
            src_ref=terms.at[g, peer],
            dst_ref=arrived.at[g, peer],
            send_sem=term_send.at[g, peer],
            recv_sem=term_recv.at[g, peer],
            device_id=(section, peer),
            device_id_type=MESH,
        )

    def dq_out(g, c):
        return pltpu.make_async_remote_copy(
            src_ref=dq.at[g, c],
            dst_ref=up_hbm.at[0, :, columns(core, g)],
            send_sem=dq_send.at[g, c],
            recv_sem=dq_recv.at[g, core],
            device_id=(section - 1, chip_first + c),
            device_id_type=MESH,
        )

    def dq_in(g, c):
        return pltpu.make_async_remote_copy(
            src_ref=dq.at[g, c],
            dst_ref=up_hbm.at[0, :, columns(c, g)],
            send_sem=dq_send.at[g, c],
            recv_sem=dq_recv.at[g, c],
            device_id=(section + 1, chip_first + c),
            device_id_type=MESH,
        )

    own_bias().wait()
    swap_bias().wait()
    scale = 1.0 / HD**0.5

    @pl.loop(0, groups)
    def _(g):
        for which in range(2):
            own_copy(which, g).wait()
            swap(which, g).wait()

        @pl.loop(1, count)
        def _(step):
            kv_in(g, lax.rem(me + step, count)).wait_recv()

        for h in range(wide // HD):
            hs = slice(h * HD, (h + 1) * HD)
            k2 = kv[g, :, 0, :, hs].reshape(count * pool, HD)
            v2 = kv[g, :, 1, :, hs].reshape(count * pool, HD)
            dk = dv = None
            for c in range(2):
                qc = qd[g, 0, c, :, hs]
                dc = qd[g, 1, c, :, hs]
                scores = dot(k2, qc, ((1,), (1,))).reshape(count, pool, tokens)
                scores = (scores + bias[c][:, None, :]).reshape(count * pool, tokens)
                top = jnp.max(scores, axis=0, keepdims=True)
                expo = jnp.exp2((scores - top) * (scale * LOG2E))
                probs = expo * (1.0 / jnp.sum(expo, axis=0, keepdims=True))
                low = probs.astype(jnp.bfloat16)
                dprob = dot(v2, dc, ((1,), (1,)))
                delta = jnp.sum(low.astype(jnp.float32) * dprob, axis=0, keepdims=True)
                sgrad = (probs * (dprob - delta) * scale).astype(jnp.bfloat16)
                dkc = dot(sgrad, qc, ((1,), (0,)))
                dvc = dot(low, dc, ((1,), (0,)))
                dk = dkc if dk is None else dk + dkc
                dv = dvc if dv is None else dv + dvc
                dq[g, c, :, hs] = dot(k2, sgrad, ((0,), (0,))).T.astype(jnp.bfloat16)
            terms[g, :, 0, :, hs] = dk.astype(jnp.bfloat16).reshape(count, pool, HD)
            terms[g, :, 1, :, hs] = dv.astype(jnp.bfloat16).reshape(count, pool, HD)

        @pl.loop(1, count)
        def _(step):
            term_out(g, lax.rem(me + step, count)).start()

        @pl.when(section > 0)
        def _():
            for c in range(2):
                dq_out(g, c).start()

        arrived[g, me] = terms[g, me]

    def grad_out(which, half, g):
        dst = (kg_hbm, vg_hbm)[which]
        return pltpu.make_async_copy(
            kin.at[which, :, columns(half, g)], dst.at[0, :, columns(half, g)], out_sem.at[which, half, g]
        )

    @pl.loop(0, groups)
    def _(g):
        @pl.loop(1, count)
        def _(step):
            term_in(g, lax.rem(me + step, count)).wait_recv()

        spread = pool_matrix((tokens, pool), 0, 1.0)
        for half in range(2):
            for which in range(2):
                total = arrived[g, half, which].astype(jnp.float32)
                for peer in range(half + 2, count, 2):
                    total = total + arrived[g, peer, which].astype(jnp.float32)
                grad = (total / 4.0).astype(jnp.bfloat16)
                kin[which, :, columns(half, g)] = dot(spread, grad, ((1,), (0,))).astype(jnp.bfloat16)
                grad_out(which, half, g).start()

    @pl.when(section == sections - 1)
    def _():
        qd[0, 0, 0] = jnp.zeros((tokens, wide), jnp.bfloat16)

        def zero_out(g, half):
            return pltpu.make_async_copy(qd.at[0, 0, 0], up_hbm.at[0, :, columns(half, g)], dq_recv.at[g, half])

        for half in range(2):
            for g in range(groups):
                zero_out(g, half).start()
        for half in range(2):
            for g in range(groups):
                zero_out(g, half).wait()

    @pl.loop(0, groups)
    def _(g):
        for which in range(2):
            for half in range(2):
                grad_out(which, half, g).wait()

        @pl.loop(1, count)
        def _(step):
            peer = lax.rem(me + step, count)
            kv_out(g, peer).wait_send()
            term_out(g, peer).wait_send()

        @pl.when(section > 0)
        def _():
            for c in range(2):
                dq_out(g, c).wait_send()

        @pl.when(section < sections - 1)
        def _():
            for c in range(2):
                dq_in(g, c).wait_recv()


def shards(query, key, value, out_grad, tile_mask):
    _, tokens, width = query.shape
    sections = lax.axis_size("section")
    count = lax.axis_size("ctx")
    pool = tokens // 4
    half_heads = width // HD // 2
    per_group = 2 if half_heads % 2 == 0 else 1
    groups = half_heads // per_group
    wide = per_group * HD
    allowed = jnp.repeat(tile_mask.T, tokens // 2, axis=1) > 0
    bias = jnp.where(allowed, 0.0, -1e30).astype(jnp.float32)
    any_spec = pl.BlockSpec(memory_space=pltpu.HBM)
    dma = pltpu.SemaphoreType.DMA
    low = jnp.bfloat16
    whole = jax.ShapeDtypeStruct(query.shape, low)
    return pl.pallas_call(
        functools.partial(kernel, sections, count, groups, wide),
        out_shape=(whole, whole, whole),
        in_specs=[any_spec] * 5,
        out_specs=(any_spec,) * 3,
        scratch_shapes=[
            pltpu.VMEM((2, tokens, width), low),
            pltpu.VMEM((2, groups, 2, pool, wide), low),
            pltpu.VMEM((groups, count, 2, pool, wide), low),
            pltpu.VMEM((groups, 2, 2, tokens, wide), low),
            pltpu.VMEM((2,) + bias.shape, jnp.float32),
            pltpu.VMEM((groups, count, 2, pool, wide), low),
            pltpu.VMEM((groups, count, 2, pool, wide), low),
            pltpu.VMEM((groups, 2, tokens, wide), low),
            dma((2, 2, groups)),
            dma((2, groups)),
            dma,
            dma((2, groups)),
            dma((2, groups)),
            dma((2,)),
            dma((groups, count)),
            dma((groups, count)),
            dma((groups, count)),
            dma((groups, count)),
            dma((groups, 2)),
            dma((groups, 2)),
            dma((2, 2, groups)),
        ],
        compiler_params=pltpu.CompilerParams(
            collective_id=0, has_side_effects=True, vmem_limit_bytes=60 * 1024 * 1024
        ),
    )(query, key, value, out_grad, bias)


def solution(mesh):
    spec = P("section", "ctx", None)
    return jax.shard_map(
        shards,
        mesh=mesh,
        in_specs=(spec, spec, spec, spec, P("ctx", None)),
        out_specs=(spec, spec, spec),
        check_vma=False,
    )
```

time: 488 us -> 122 us (0.25)
  matrix products: 188 us -> 0 us
  waiting for transfers between devices: 135 us -> 0 us
  Pallas kernels: 0 us -> 112 us
  local copies, waits for them, and re-layouts: 69.6 us -> 8.14 us
  other arithmetic: 59.3 us -> 0.68 us
  loops' own time: 16.2 us -> 0 us
  between operations: 13.9 us -> 0.65 us
    dot_general x98 -> x0, matrix products: 188 us -> none  [the longest x24 54.4 us: head_core(): dprob = jnp.dot(dhead, vhead.T, preferred_element_type=jnp.float32)]
    pallas_call x0 -> x1, Pallas kernels: none -> 112 us  [shards(): pl.pallas_call(functools.partial(kernel, sections, count, groups, wide),...]
    all_gather x2 -> x0, waiting for transfers between devices: 62.4 us -> none  [the longest x1 40.7 us: shards(): lax.all_gather(pool_band(local_v, row_len), 'ctx', axis=0, tiled=True)]
    ppermute x1 -> x0, waiting for transfers between devices: 53 us -> none  [from_behind(): lax.ppermute(value, axis, [(source, source + steps) for source in range(f...]
    dynamic_update_slice x24 -> x0, other arithmetic: 26.9 us -> none  [shards(): lax.map(per_head_kept, jnp.arange(heads, dtype=jnp.int32))]
    reduce_sum x26 -> x0, other arithmetic: 19.9 us -> none  [the longest x2 11.4 us: pool_band(): grid.mean(axis=(1, 3)).reshape(-1, data.shape[1]).astype(jnp.bfloat16)]
    reduce_scatter x1 -> x0, waiting for transfers between devices: 19.8 us -> none  [shards(): lax.psum_scatter(jnp.concatenate([kpart.reshape(row_len // 2 * lax.axis_s...]
    another operation x1 -> x0, loops' own time: 16.2 us -> none  [shards(): lax.map(per_head_kept, jnp.arange(heads, dtype=jnp.int32))]
  transfers between devices with their start and end apart: 4 -> 0, of which waited for: 4 -> 0; matrix products, arithmetic and copies ran while one was open for 4% -> 0% of each run, Pallas kernels for 0% -> 0%
where the time goes in v1:
time: 122 us; the launch traced here: 121 us
  Pallas kernels  112 us (92%)
  local copies, waits for them, and re-layouts  8.14 us (7%)
    pallas_call x1, Pallas kernels, shards(): pl.pallas_call(functools.partial(kernel, sections, count, groups, wide),...  112 us
    unnamed x7, local copies, waits for them, and re-layouts  7.3 us

profile of v1, /device:TPU:1, one launch (start us, length us, event | category | flops | bytes accessed | tf_op | source)
XLA Modules:
  0.0 121.0 jit_solution(4303564067271905015)
XLA Ops:
  0.6 0.7 fusion
  1.3 0.1 copy.8
  1.4 0.1 broadcast_in_dim.13
  1.5 0.7 select_n.10.bias_hbm
  2.2 111.6 %shard_map.76 = (bf16[1,384,3072]{2,1,0:T(8,128)(2,1)}, bf16[1,384,3072]{2,1,0:T(8,128)(2,1)}, bf16[1,384,3072]{2,1,0:T(8,128)(2,1)}) custom-call(bf16[1,384,3072]{2,1,0:T(8,128)(2,1)} %q_hbm.1, bf16[1,384,3072]{2,1,0:T(8,128)(2,1)} %k_hbm.1, bf16[1,384,3072]{2,1,0:T(8,128)(2,1)} %v_hbm.1, bf16[1,384,3072]{2,1,0:T(8,128)(2,1)} %d_hbm.1, ...), custom_call_target="tpu_custom_call" | custom-call | tf_op jit(solution)/shard_map/pallas_call | solution.py:316
  113.7 0.0 copy-start.1
  113.7 3.4 %copy.12 = bf16[1,384,3072]{2,1,0:T(8,128)(2,1)} copy(bf16[1,384,3072]{2,1,0:T(8,128)(2,1)} %get-tuple-element.6) | data formatting | bytes 4718592
  117.1 0.0 copy-done.1
  117.1 0.0 copy-start
  117.1 1.4 %copy.13 = bf16[1,384,3072]{2,1,0:T(8,128)(2,1)} copy(bf16[1,384,3072]{2,1,0:T(8,128)(2,1)S(1)} %copy-done.1) | data formatting | bytes 4718592
  118.5 1.1 copy-done
  119.6 1.4 %copy.14 = bf16[1,384,3072]{2,1,0:T(8,128)(2,1)} copy(bf16[1,384,3072]{2,1,0:T(8,128)(2,1)S(1)} %copy-done) | data formatting | bytes 4718592
Async XLA Ops:
  113.7 3.4 %copy-start.1 = (bf16[1,384,3072]{2,1,0:T(8,128)(2,1)S(1)}, bf16[1,384,3072]{2,1,0:T(8,128)(2,1)}, u32[]{:S(2)}) copy-start(bf16[1,384,3072]{2,1,0:T(8,128)(2,1)} %get-tuple-element.7) | copy-start | bytes 7077892
  117.1 2.5 %copy-start = (bf16[1,384,3072]{2,1,0:T(8,128)(2,1)S(1)}, bf16[1,384,3072]{2,1,0:T(8,128)(2,1)}, u32[]{:S(2)}) copy-start(bf16[1,384,3072]{2,1,0:T(8,128)(2,1)} %get-tuple-element.8) | copy-start | bytes 7077892

commit v2 on v1

--- a/solution.py
+++ b/solution.py
@@ -10,6 +10,7 @@
 HD = 128
 MESH = pl.DeviceIdType.MESH
 LOG2E = 1.4426950408889634
+AHEAD = 2
 
 
 def dot(a, b, dims):
@@ -18,11 +19,12 @@
 
 def kernel(
     sections, count, groups, wide,
-    q_hbm, k_hbm, v_hbm, d_hbm, bias_hbm,
-    kg_hbm, vg_hbm, up_hbm,
-    kin, pooled, kv, qd, bias, terms, arrived, dq,
-    in_sem, own_sem, own_bias_sem, swap_send, swap_recv, bias_sems,
-    kv_send, kv_recv, term_send, term_recv, dq_send, dq_recv, out_sem,
+    q_hbm, k_hbm, v_hbm, d_hbm, mask_hbm,
+    pg_hbm, up_hbm,
+    kin, pooled, kv, qd, mask, bias, terms, arrived, relayed, dq, grads,
+    in_sem, own_sem, mask_sem, swap_send, swap_recv, bias_sems,
+    kv_send, kv_recv, pass_send, pass_recv, term_send, term_recv, relay_send, relay_recv,
+    dq_send, dq_recv, out_sem,
 ):
     tokens = qd.shape[3]
     row_len = tokens // 2
@@ -32,6 +34,11 @@
     core = lax.rem(me, 2)
     chip_first = me - core
     partner = chip_first + 1 - core
+    relay = count == 8
+    across = lax.rem(me // 2, 2)
+    beside_x = chip_first + 2 - 4 * across
+    beside_y = chip_first + 4 - 8 * (me // 4)
+    corner = 2 * (count // 2 - 1) - chip_first
 
     def columns(half, g):
         return pl.ds(pl.multiple_of((half * groups + g) * wide, wide), wide)
@@ -46,8 +53,8 @@
         src = (q_hbm, d_hbm)[which]
         return pltpu.make_async_copy(src.at[0, :, columns(core, g)], qd.at[g, which, core], own_sem.at[which, g])
 
-    def own_bias():
-        return pltpu.make_async_copy(bias_hbm, bias.at[core], own_bias_sem)
+    def own_mask():
+        return pltpu.make_async_copy(mask_hbm, mask, mask_sem)
 
     @pl.loop(0, groups)
     def _(g):
@@ -60,7 +67,14 @@
         for which in range(2):
             own_copy(which, g).start()
 
-    own_bias().start()
+    own_mask().start()
+
+    own_mask().wait()
+    tile = lax.broadcasted_iota(jnp.int32, (2, tokens), 0)
+    token = lax.broadcasted_iota(jnp.int32, (2, tokens), 1)
+    inside = jnp.where((token >= row_len) == (tile == 1), 1.0, 0.0)
+    reads = dot(mask[...].astype(jnp.float32), inside, ((0,), (0,)))
+    bias[core] = jnp.where(reads > 0.5, 0.0, -1e30)
 
     barrier = pltpu.get_barrier_semaphore()
     for step in range(1, count):
@@ -94,20 +108,13 @@
 
     def swap_bias():
         return pltpu.make_async_remote_copy(
-            src_ref=bias_hbm,
+            src_ref=bias.at[core],
             dst_ref=bias.at[core],
             send_sem=bias_sems.at[0],
             recv_sem=bias_sems.at[1],
             device_id=(section, partner),
             device_id_type=MESH,
         )
-
-    swap_bias().start()
-
-    @pl.loop(0, groups)
-    def _(g):
-        for which in range(2):
-            swap(which, g).start()
 
     def kv_out(g, peer):
         return pltpu.make_async_remote_copy(
@@ -135,8 +142,30 @@
         cell = lax.broadcasted_iota(jnp.int32, shape, 1 - token_dim)
         return jnp.where((token >> 1) == cell, value, 0.0).astype(jnp.bfloat16)
 
-    @pl.loop(0, groups)
-    def _(g):
+    def passed(g, which, j):
+        src = ((beside_x, beside_y)[which]) + j
+        dst = ((beside_y, beside_x)[which]) + core
+        return pltpu.make_async_remote_copy(
+            src_ref=kv.at[g, src, which],
+            dst_ref=kv.at[g, src, which],
+            send_sem=pass_send.at[g, which, j],
+            recv_sem=pass_recv.at[g, which, j],
+            device_id=(section, dst),
+            device_id_type=MESH,
+        )
+
+    def each_peer(act):
+        if relay:
+            for j in range(2):
+                act(beside_x + j)
+                act(beside_y + j)
+            act(partner)
+        else:
+            @pl.loop(1, count)
+            def _(step):
+                act(lax.rem(me + step, count))
+
+    def pool_group(g):
         mean = pool_matrix((pool, tokens), 1, 0.25)
         for half in range(2):
             for which in range(2):
@@ -145,29 +174,83 @@
                 pooled[half, g, which] = block.astype(jnp.bfloat16)
         kv[g, me] = pooled[core, g]
 
-        @pl.loop(1, count)
-        def _(step):
-            kv_out(g, lax.rem(me + step, count)).start()
-
-    def term_out(g, peer):
-        return pltpu.make_async_remote_copy(
-            src_ref=terms.at[g, peer],
-            dst_ref=arrived.at[g, me],
-            send_sem=term_send.at[g, peer],
-            recv_sem=term_recv.at[g, me],
+    def send_group(g):
+        each_peer(lambda peer: kv_out(g, peer).start())
+        for which in range(2):
+            swap(which, g).start()
+
+    def pass_group(g):
+        each_peer(lambda peer: kv_in(g, peer).wait_recv())
+        if relay:
+            for which in range(2):
+                for j in range(2):
+                    passed(g, which, j).start()
+
+    ahead = min(AHEAD, groups)
+    swap_bias().start()
+    for g in range(ahead):
+        pool_group(g)
+        send_group(g)
+
+    @pl.loop(ahead, groups)
+    def _(g):
+        pool_group(g)
+
+    pass_group(0)
+
+    def term_out(g, peer, which):
+        return pltpu.make_async_remote_copy(
+            src_ref=terms.at[g, peer, which],
+            dst_ref=arrived.at[g, me, which],
+            send_sem=term_send.at[g, peer, which],
+            recv_sem=term_recv.at[g, me, which],
             device_id=(section, peer),
             device_id_type=MESH,
         )
 
-    def term_in(g, peer):
-        return pltpu.make_async_remote_copy(
-            src_ref=terms.at[g, peer],
-            dst_ref=arrived.at[g, peer],
-            send_sem=term_send.at[g, peer],
-            recv_sem=term_recv.at[g, peer],
+    def term_in(g, peer, which):
+        return pltpu.make_async_remote_copy(
+            src_ref=terms.at[g, peer, which],
+            dst_ref=arrived.at[g, peer, which],
+            send_sem=term_send.at[g, peer, which],
+            recv_sem=term_recv.at[g, peer, which],
             device_id=(section, peer),
             device_id_type=MESH,
         )
+
+    def relay_out(g, which, j):
+        return pltpu.make_async_remote_copy(
+            src_ref=terms.at[g, corner + j, which],
+            dst_ref=relayed.at[g, which, j],
+            send_sem=relay_send.at[g, which, j],
+            recv_sem=relay_recv.at[g, which, j],
+            device_id=(section, ((beside_x, beside_y)[which]) + core),
+            device_id_type=MESH,
+        )
+
+    def combine(g):
+        for which in range(2):
+            for j in range(2):
+                relay_out(g, which, j).wait_recv()
+                peer = ((beside_y, beside_x)[which]) + j
+                both = terms[g, peer, which].astype(jnp.float32) + relayed[g, which, j].astype(jnp.float32)
+                terms[g, peer, which] = both.astype(jnp.bfloat16)
+                term_out(g, peer, which).start()
+
+    def send_terms(g):
+        if relay:
+            for which in range(2):
+                for j in range(2):
+                    relay_out(g, which, j).start()
+            for which in range(2):
+                for j in range(2):
+                    term_out(g, ((beside_x, beside_y)[which]) + j, which).start()
+                term_out(g, partner, which).start()
+        else:
+            @pl.loop(1, count)
+            def _(step):
+                for which in range(2):
+                    term_out(g, lax.rem(me + step, count), which).start()
 
     def dq_out(g, c):
         return pltpu.make_async_remote_copy(
@@ -189,7 +272,6 @@
             device_id_type=MESH,
         )
 
-    own_bias().wait()
     swap_bias().wait()
     scale = 1.0 / HD**0.5
 
@@ -199,9 +281,14 @@
             own_copy(which, g).wait()
             swap(which, g).wait()
 
-        @pl.loop(1, count)
-        def _(step):
-            kv_in(g, lax.rem(me + step, count)).wait_recv()
+        if relay:
+            for which in range(2):
+                for j in range(2):
+                    passed(g, which, j).wait_recv()
+
+        @pl.when(g + ahead < groups)
+        def _():
+            send_group(g + ahead)
 
         for h in range(wide // HD):
             hs = slice(h * HD, (h + 1) * HD)
@@ -227,10 +314,17 @@
                 dq[g, c, :, hs] = dot(k2, sgrad, ((0,), (0,))).T.astype(jnp.bfloat16)
             terms[g, :, 0, :, hs] = dk.astype(jnp.bfloat16).reshape(count, pool, HD)
             terms[g, :, 1, :, hs] = dv.astype(jnp.bfloat16).reshape(count, pool, HD)
-
-        @pl.loop(1, count)
-        def _(step):
-            term_out(g, lax.rem(me + step, count)).start()
+            if h == 0:
+                @pl.when(g + 1 < groups)
+                def _():
+                    pass_group(g + 1)
+
+                if relay:
+                    @pl.when(g > 0)
+                    def _():
+                        combine(g - 1)
+
+        send_terms(g)
 
         @pl.when(section > 0)
         def _():
@@ -239,27 +333,24 @@
 
         arrived[g, me] = terms[g, me]
 
-    def grad_out(which, half, g):
-        dst = (kg_hbm, vg_hbm)[which]
-        return pltpu.make_async_copy(
-            kin.at[which, :, columns(half, g)], dst.at[0, :, columns(half, g)], out_sem.at[which, half, g]
-        )
+    if relay:
+        combine(groups - 1)
+
+    def grad_out(half, g):
+        return pltpu.make_async_copy(grads.at[half, g], pg_hbm.at[:, :, columns(half, g)], out_sem.at[half, g])
 
     @pl.loop(0, groups)
     def _(g):
-        @pl.loop(1, count)
-        def _(step):
-            term_in(g, lax.rem(me + step, count)).wait_recv()
-
-        spread = pool_matrix((tokens, pool), 0, 1.0)
+        each_peer(lambda peer: [term_in(g, peer, which).wait_recv() for which in range(2)])
         for half in range(2):
-            for which in range(2):
-                total = arrived[g, half, which].astype(jnp.float32)
-                for peer in range(half + 2, count, 2):
-                    total = total + arrived[g, peer, which].astype(jnp.float32)
-                grad = (total / 4.0).astype(jnp.bfloat16)
-                kin[which, :, columns(half, g)] = dot(spread, grad, ((1,), (0,))).astype(jnp.bfloat16)
-                grad_out(which, half, g).start()
+            if relay:
+                peers = [chip_first + half, beside_x + half, beside_y + half]
+            else:
+                peers = range(half, count, 2)
+            for which in range(2):
+                total = sum(arrived[g, peer, which].astype(jnp.float32) for peer in peers)
+                grads[half, g, which] = (total / 4.0).astype(jnp.bfloat16)
+            grad_out(half, g).start()
 
     @pl.when(section == sections - 1)
     def _():
@@ -277,15 +368,15 @@
 
     @pl.loop(0, groups)
     def _(g):
-        for which in range(2):
-            for half in range(2):
-                grad_out(which, half, g).wait()
-
-        @pl.loop(1, count)
-        def _(step):
-            peer = lax.rem(me + step, count)
-            kv_out(g, peer).wait_send()
-            term_out(g, peer).wait_send()
+        for half in range(2):
+            grad_out(half, g).wait()
+        each_peer(lambda peer: kv_out(g, peer).wait_send())
+        each_peer(lambda peer: [term_out(g, peer, which).wait_send() for which in range(2)])
+        if relay:
+            for which in range(2):
+                for j in range(2):
+                    passed(g, which, j).wait_send()
+                    relay_out(g, which, j).wait_send()
 
         @pl.when(section > 0)
         def _():
@@ -296,6 +387,18 @@
         def _():
             for c in range(2):
                 dq_in(g, c).wait_recv()
+
+
+def spread_kernel(pooled_grads, given, key_grad, value_grad, upstream):
+    tokens = given.shape[1]
+    shape = (tokens, tokens // 4)
+    token = lax.broadcasted_iota(jnp.int32, shape, 0)
+    token = jnp.where(token >= tokens // 2, token - tokens // 2, token)
+    cell = lax.broadcasted_iota(jnp.int32, shape, 1)
+    spread = jnp.where((token >> 1) == cell, 1.0, 0.0).astype(jnp.bfloat16)
+    key_grad[0] = dot(spread, pooled_grads[0], ((1,), (0,))).astype(jnp.bfloat16)
+    value_grad[0] = dot(spread, pooled_grads[1], ((1,), (0,))).astype(jnp.bfloat16)
+    upstream[...] = given[...]
 
 
 def shards(query, key, value, out_grad, tile_mask):
@@ -304,29 +407,31 @@
     count = lax.axis_size("ctx")
     pool = tokens // 4
     half_heads = width // HD // 2
-    per_group = 2 if half_heads % 2 == 0 else 1
+    per_group = max(n for n in (1, 2, 3) if half_heads % n == 0)
     groups = half_heads // per_group
     wide = per_group * HD
-    allowed = jnp.repeat(tile_mask.T, tokens // 2, axis=1) > 0
-    bias = jnp.where(allowed, 0.0, -1e30).astype(jnp.float32)
     any_spec = pl.BlockSpec(memory_space=pltpu.HBM)
     dma = pltpu.SemaphoreType.DMA
     low = jnp.bfloat16
     whole = jax.ShapeDtypeStruct(query.shape, low)
-    return pl.pallas_call(
+    tiles = tile_mask.shape[1]
+    pooled_grads, upstream = pl.pallas_call(
         functools.partial(kernel, sections, count, groups, wide),
-        out_shape=(whole, whole, whole),
+        out_shape=(jax.ShapeDtypeStruct((2, pool, width), low), whole),
         in_specs=[any_spec] * 5,
-        out_specs=(any_spec,) * 3,
+        out_specs=(any_spec,) * 2,
         scratch_shapes=[
             pltpu.VMEM((2, tokens, width), low),
             pltpu.VMEM((2, groups, 2, pool, wide), low),
             pltpu.VMEM((groups, count, 2, pool, wide), low),
             pltpu.VMEM((groups, 2, 2, tokens, wide), low),
-            pltpu.VMEM((2,) + bias.shape, jnp.float32),
+            pltpu.VMEM(tile_mask.shape, jnp.int32),
+            pltpu.VMEM((2, tiles, tokens), jnp.float32),
             pltpu.VMEM((groups, count, 2, pool, wide), low),
             pltpu.VMEM((groups, count, 2, pool, wide), low),
+            pltpu.VMEM((groups, 2, 2, pool, wide), low),
             pltpu.VMEM((groups, 2, tokens, wide), low),
+            pltpu.VMEM((2, groups, 2, pool, wide), low),
             dma((2, 2, groups)),
             dma((2, groups)),
             dma,
@@ -335,16 +440,29 @@
             dma((2,)),
             dma((groups, count)),
             dma((groups, count)),
-            dma((groups, count)),
-            dma((groups, count)),
+            dma((groups, 2, 2)),
+            dma((groups, 2, 2)),
+            dma((groups, count, 2)),
+            dma((groups, count, 2)),
+            dma((groups, 2, 2)),
+            dma((groups, 2, 2)),
             dma((groups, 2)),
             dma((groups, 2)),
-            dma((2, 2, groups)),
+            dma((2, groups)),
         ],
         compiler_params=pltpu.CompilerParams(
             collective_id=0, has_side_effects=True, vmem_limit_bytes=60 * 1024 * 1024
         ),
-    )(query, key, value, out_grad, bias)
+    )(query, key, value, out_grad, tile_mask)
+    band = min(width, 4 * wide)
+    block = pl.BlockSpec((1, tokens, band), lambda i: (0, 0, i))
+    return pl.pallas_call(
+        spread_kernel,
+        grid=(width // band,),
+        out_shape=(whole, whole, whole),
+        in_specs=[pl.BlockSpec((2, pool, band), lambda i: (0, 0, i)), block],
+        out_specs=(block,) * 3,
+    )(pooled_grads, upstream)
 
 
 def solution(mesh):

time: 122 us -> 99 us (0.81)
  Pallas kernels: 112 us -> 98.2 us
  local copies, waits for them, and re-layouts: 8.14 us -> 0 us
    pallas_call x1, Pallas kernels: 112 us -> 93.3 us  [shards(): pl.pallas_call(functools.partial(kernel, sections, count, groups, wide),...]
    unnamed x7 -> x0, local copies, waits for them, and re-layouts: 7.3 us -> none
    pallas_call x0 -> x1, Pallas kernels: none -> 4.84 us  [shards(): pl.pallas_call(spread_kernel, grid=(width // band,), out_shape=(whole, wh...]
where the time goes in v2:
time: 99 us; the launch traced here: 98.8 us
  Pallas kernels  98.2 us (99%)
    pallas_call x1, Pallas kernels, shards(): pl.pallas_call(functools.partial(kernel, sections, count, groups, wide),...  93.3 us
    pallas_call x1, Pallas kernels, shards(): pl.pallas_call(spread_kernel, grid=(width // band,), out_shape=(whole, wh...  4.84 us

profile of v2, /device:TPU:1, one launch (start us, length us, event | category | flops | bytes accessed | tf_op | source)
XLA Modules:
  0.0 98.8 jit_solution(4336041178101910783)
XLA Ops:
  0.6 93.3 %shard_map.76 = (bf16[2,96,3072]{2,1,0:T(8,128)(2,1)}, bf16[1,384,3072]{2,1,0:T(8,128)(2,1)}) custom-call(bf16[1,384,3072]{2,1,0:T(8,128)(2,1)} %q_hbm.1, bf16[1,384,3072]{2,1,0:T(8,128)(2,1)} %k_hbm.1, bf16[1,384,3072]{2,1,0:T(8,128)(2,1)} %v_hbm.1, bf16[1,384,3072]{2,1,0:T(8,128)(2,1)} %d_hbm.1, s32[2,8]{1,0:T(2,128)} %mask_hbm.1), custom_call_target="tpu_custom_call" | custom-call | tf_op jit(solution)/shard_map/pallas_call | solution.py:418
  94.0 4.8 %shard_map.77 = (bf16[1,384,3072]{2,1,0:T(8,128)(2,1)}, bf16[1,384,3072]{2,1,0:T(8,128)(2,1)}, bf16[1,384,3072]{2,1,0:T(8,128)(2,1)}) custom-call(bf16[2,96,3072]{2,1,0:T(8,128)(2,1)} %get-tuple-element.5.pooled_grads, bf16[1,384,3072]{2,1,0:T(8,128)(2,1)} %get-tuple-element.6.given), custom_call_target="tpu_custom_call" | custom-call | tf_op jit(solution)/shard_map/pallas_call | solution.py:459

commit v3 on v2

--- a/solution.py
+++ b/solution.py
@@ -454,7 +454,7 @@
             collective_id=0, has_side_effects=True, vmem_limit_bytes=60 * 1024 * 1024
         ),
     )(query, key, value, out_grad, tile_mask)
-    band = min(width, 4 * wide)
+    band = 2 * wide
     block = pl.BlockSpec((1, tokens, band), lambda i: (0, 0, i))
     return pl.pallas_call(
         spread_kernel,

time: 99 us -> 100 us (1.010)
  Pallas kernels: 98.2 us -> 99.2 us
where the time goes in v3:
time: 100 us; the launch traced here: 99.8 us
  Pallas kernels  99.2 us (99%)
    pallas_call x1, Pallas kernels, shards(): pl.pallas_call(functools.partial(kernel, sections, count, groups, wide),...  93.3 us
    pallas_call x1, Pallas kernels, shards(): pl.pallas_call(spread_kernel, grid=(width // band,), out_shape=(whole, wh...  5.84 us

profile of v3, /device:TPU:1, one launch (start us, length us, event | category | flops | bytes accessed | tf_op | source)
XLA Modules:
  0.0 99.8 jit_solution(11484175418759175297)
XLA Ops:
  0.6 93.3 %shard_map.76 = (bf16[2,96,3072]{2,1,0:T(8,128)(2,1)}, bf16[1,384,3072]{2,1,0:T(8,128)(2,1)}) custom-call(bf16[1,384,3072]{2,1,0:T(8,128)(2,1)} %q_hbm.1, bf16[1,384,3072]{2,1,0:T(8,128)(2,1)} %k_hbm.1, bf16[1,384,3072]{2,1,0:T(8,128)(2,1)} %v_hbm.1, bf16[1,384,3072]{2,1,0:T(8,128)(2,1)} %d_hbm.1, s32[2,8]{1,0:T(2,128)} %mask_hbm.1), custom_call_target="tpu_custom_call" | custom-call | tf_op jit(solution)/shard_map/pallas_call | solution.py:418
  94.0 5.8 %shard_map.77 = (bf16[1,384,3072]{2,1,0:T(8,128)(2,1)}, bf16[1,384,3072]{2,1,0:T(8,128)(2,1)}, bf16[1,384,3072]{2,1,0:T(8,128)(2,1)}) custom-call(bf16[2,96,3072]{2,1,0:T(8,128)(2,1)} %get-tuple-element.5.pooled_grads, bf16[1,384,3072]{2,1,0:T(8,128)(2,1)} %get-tuple-element.6.given), custom_call_target="tpu_custom_call" | custom-call | tf_op jit(solution)/shard_map/pallas_call | solution.py:459
